TPU v7x, 256 devices: a whole 4x4x8 slice. The times are simulated.
256 devices in a mesh: band: 64 (over z_lo, x, y, core), sector: 4 (over z_hi).
Axes of the slice: x: 4, y: 4, z: 8 (z_hi: 4, z_lo: 2; z = z_hi * 2 + z_lo), core: 2. Of those that a mesh axis runs over, the one named last changes fastest.
Arguments:
- field: bfloat16 [64, 1440, 72], P('band', 'sector'), may hold values from -6 to 6
- filters: float32 [9, 64, 3, 17], P(None, 'band'), may hold values from -1.2 to 1.2
- reach: int32 [64], P('band'), may hold values from 1 to 8, as said below
- w_enc: bfloat16 [9, 72, 384], replicated, may hold values from -0.25 to 0.25
- gain: float32 [384], replicated, may hold values from 0.5 to 1.5
- w_qkv: bfloat16 [384, 1152], replicated, may hold values from -0.3125 to 0.3125
- w_out: bfloat16 [384, 384], replicated, may hold values from -0.3125 to 0.3125
- tau: float32 [8], replicated, may hold values from 0.25 to 24
- neighbours: int32 [64, 4, 3, 4], P('band', 'sector'), may hold values from 0 to 1, as said below
Outputs:
- output: bfloat16 [64, 1440, 384], P('band', 'sector')
Inputs may be any that keep to these rules, and one draw needn't show every extreme that they name: reach[i] is the filter's longitude reach in row i; it equals 8 in the first and last row. neighbours[b, s, r, t] is 1 where query block (b, s) attends key row b - 1 + r in sector t; it is 1 for the block's own rows in its own sector and 0 for rows outside the grid.
All inputs are finite; a program needn't handle non-finite values.
Results may differ from a plain program's by a relative error of at most 0.03.
Values may be sent and summed in bfloat16 or wider, within the bound.
No kernel may reach another device: no remote copies, remote signals or barrier semaphores. Data moves between devices by JAX's collectives and lax.ppermute only.
A program may use at most 64 MiB of HBM per device.

v0:
```python
import math
import jax
import jax.numpy as jnp
from jax import lax
from jax.sharding import PartitionSpec as P

HEADS = 8
FR = 1
LW = 8
KH = 1


def padded(block, sides, width, periodic):
    for axis, dim in sides:
        count = lax.axis_size(axis)
        forward = [(i, i + 1) for i in range(count - 1)]
        if periodic:
            forward.append((count - 1, 0))
        backward = [(target, source) for source, target in forward]
        low = lax.ppermute(
            lax.slice_in_dim(block, block.shape[dim] - width, None, axis=dim), axis, forward
        )
        high = lax.ppermute(lax.slice_in_dim(block, 0, width, axis=dim), axis, backward)
        block = jnp.concatenate([low, block, high], axis=dim)
    return block


def rotate(values, row_ids, col_ids, nlat, nlon):
    npair = values.shape[-1] // 2
    nhalf = npair // 2
    index = jnp.arange(npair, dtype=jnp.int32)
    lon_freq = jnp.where(index < nhalf, index + 1, 0).astype(jnp.float32)
    lat_freq = jnp.where(index >= nhalf, index - nhalf + 1, 0).astype(jnp.float32)
    lon_angle = 2.0 * math.pi / nlon * col_ids.astype(jnp.float32)
    lat_angle = math.pi / nlat * (row_ids.astype(jnp.float32) + 0.5)
    angle = lat_angle[:, None, None] * lat_freq + lon_angle[None, :, None] * lon_freq
    cosine = jnp.cos(angle)[:, :, None, :]
    sine = jnp.sin(angle)[:, :, None, :]
    first = values[..., :npair]
    second = values[..., npair:]
    return jnp.concatenate([first * cosine - second * sine, first * sine + second * cosine], -1)


def normalize(hidden, gain):
    values = hidden.astype(jnp.float32)
    meansquare = jnp.mean(values * values, -1, keepdims=True)
    return (values * lax.rsqrt(meansquare + 1e-05) * gain).astype(jnp.bfloat16)


def spread(payload):
    cycle_cells = lax.all_gather(payload, "sector", axis=1, tiled=True)
    return padded(cycle_cells, (("band", 0),), KH, False)


def local(field, filters, reach, w_enc, gain, w_qkv, w_out, tau, neighbours):
    rows_dev, lon_dev, channels = field.shape
    d_model = gain.shape[0]
    head_dim = d_model // HEADS
    nlat = rows_dev * lax.axis_size("band")
    nlon = lon_dev * lax.axis_size("sector")
    row_start = lax.axis_index("band") * rows_dev
    col_start = lax.axis_index("sector") * lon_dev
    side_cells = padded(field, (("sector", 1),), LW, True)
    block_cells = padded(side_cells, (("band", 0),), FR, False)
    offsets = jnp.abs(jnp.arange(2 * LW + 1, dtype=jnp.int32) - LW)
    tap_keep = (offsets[None, :] <= reach[:, None]).astype(jnp.float32)
    tap_weights = filters * tap_keep[None, :, None, :]
    shifted = jnp.stack(
        [
            jnp.stack(
                [
                    block_cells[above : above + rows_dev, shift : shift + lon_dev]
                    for shift in range(2 * LW + 1)
                ],
                1,
            )
            for above in range(2 * FR + 1)
        ],
        1,
    )
    conv = jnp.einsum(
        "kiab,iabjc->kijc",
        tap_weights,
        shifted.astype(jnp.float32),
        precision=lax.Precision.HIGHEST,
    ).astype(jnp.bfloat16)
    hidden = jax.nn.gelu(
        jnp.einsum("kijc,kcd->ijd", conv, w_enc, preferred_element_type=jnp.float32)
    ).astype(jnp.bfloat16)
    own_rows = row_start + jnp.arange(rows_dev, dtype=jnp.int32)
    own_cols = col_start + jnp.arange(lon_dev, dtype=jnp.int32)
    normed = normalize(hidden, gain).reshape(rows_dev * lon_dev, d_model)
    proj = jnp.dot(normed, w_qkv, preferred_element_type=jnp.float32)
    proj = proj.reshape(rows_dev, lon_dev, 3, HEADS, head_dim)
    query = rotate(proj[:, :, 0], own_rows, own_cols, nlat, nlon).astype(jnp.bfloat16)
    key_own = rotate(proj[:, :, 1], own_rows, own_cols, nlat, nlon).astype(jnp.bfloat16)
    value_own = proj[:, :, 2].astype(jnp.bfloat16)
    payload = jnp.concatenate(
        [
            key_own.reshape(rows_dev, lon_dev, d_model),
            value_own.reshape(rows_dev, lon_dev, d_model),
        ],
        -1,
    )
    gathered = spread(payload)
    key_rows = gathered.shape[0]
    key_all = gathered[..., :d_model].reshape(key_rows, nlon, HEADS, head_dim)
    value_all = gathered[..., d_model:].reshape(key_rows, nlon, HEADS, head_dim)
    keymask = jnp.repeat(neighbours[0, 0], lon_dev, axis=1).reshape(-1) > 0
    queries = jnp.transpose(query.reshape(rows_dev * lon_dev, HEADS, head_dim), (1, 0, 2))
    key_heads = jnp.transpose(key_all.reshape(key_rows * nlon, HEADS, head_dim), (1, 0, 2))
    value_heads = jnp.transpose(value_all.reshape(key_rows * nlon, HEADS, head_dim), (1, 0, 2))
    inv_root = 1.0 / math.sqrt(head_dim)

    def one_head(operands):
        q_head, k_head, v_head, temper = operands
        scores = jnp.einsum("qd,kd->qk", q_head, k_head, preferred_element_type=jnp.float32)
        scores = scores * (temper * inv_root)
        scores = jnp.where(keymask[None, :], scores, -1e30)
        peak = jnp.max(scores, -1, keepdims=True)
        expo = jnp.exp(scores - peak)
        total = jnp.sum(expo, -1, keepdims=True)
        summed = jnp.dot(expo.astype(jnp.bfloat16), v_head, preferred_element_type=jnp.float32)
        return summed / total

    attended = lax.map(one_head, (queries, key_heads, value_heads, tau))
    attended = (
        jnp.transpose(attended, (1, 0, 2)).reshape(rows_dev * lon_dev, d_model).astype(jnp.bfloat16)
    )
    mixed = jnp.dot(attended, w_out, preferred_element_type=jnp.float32).reshape(
        rows_dev, lon_dev, d_model
    )
    return (hidden.astype(jnp.float32) + mixed).astype(jnp.bfloat16)


def solution(mesh):
    return jax.shard_map(
        local,
        mesh=mesh,
        in_specs=(
            P("band", "sector", None),
            P(None, "band", None, None),
            P("band"),
            P(),
            P(),
            P(),
            P(),
            P(),
            P("band", "sector", None, None),
        ),
        out_specs=P("band", "sector", None),
        check_vma=False,
    )
```

profile of v0, /device:TPU:31, one launch (start us, length us, event | category | flops | bytes accessed | tf_op | source)
XLA Modules:
  0.0 237.7 jit_solution(11369777460939733356)
XLA Ops:
  7.4 3.0 %collective-permute-start = (bf16[1,8,72]{1,2,0:T(8,128)(2,1)S(1)}, bf16[1,8,72]{1,2,0:T(8,128)(2,1)S(1)}, u32[]{:S(2)}, u32[]{:S(2)}) collective-permute-start(bf16[1,8,72]{1,2,0:T(8,128)(2,1)S(1)} %get-tuple-element.317), channel_id=1, source_target_pairs={{0,1},{1,2},{2,3},{3,0},{4,5},{5,6},{6,7},{7,4},{8,9},{9,10},{10,1... | collective-permute-start | bytes 3464 | tf_op jit(solution)/shard_map/ppermute | solution.py:20
  10.4 3.1 %collective-permute-start.1 = (bf16[1,8,72]{1,2,0:T(8,128)(2,1)S(1)}, bf16[1,8,72]{1,2,0:T(8,128)(2,1)S(1)}, u32[]{:S(2)}, u32[]{:S(2)}) collective-permute-start(bf16[1,8,72]{1,2,0:T(8,128)(2,1)S(1)} %get-tuple-element.318), channel_id=1, source_target_pairs={{1,0},{2,1},{3,2},{0,3},{5,4},{6,5},{7,6},{4,7},{9,8},{10,9},{11,1... | collective-permute-start | bytes 3464 | tf_op jit(solution)/shard_map/ppermute | solution.py:23
  17.9 3.1 %collective-permute-start.2 = (bf16[1,376,72]{1,2,0:T(8,128)(2,1)S(1)}, bf16[1,376,72]{1,2,0:T(8,128)(2,1)S(1)}, u32[]{:S(2)}, u32[]{:S(2)}) collective-permute-start(bf16[1,376,72]{1,2,0:T(8,128)(2,1)S(1)} %pad_maximum_fusion.4), channel_id=1, source_target_pairs={{0,4},{4,8},{8,12},{12,16},{16,20},{20,24},{24,28},{28,32},{32,36}... | collective-permute-start | bytes 162440 | tf_op jit(solution)/shard_map/ppermute | solution.py:20
  36.4 2.3 fusion.30
  42.5 52.8 %all-gather.2.cloned.1.call-done = bf16[1,1440,768]{2,1,0:T(8,128)(2,1)} async-done(((bf16[1,360,768]{2,1,0:T(8,128)(2,1)}), bf16[1,1440,768]{2,1,0:T(8,128)(2,1)}) %all-gather.2.cloned.1.call-update) | async-done | bytes 2211856 | tf_op jit(solution)/shard_map/all_gather | solution.py:51
  95.3 5.2 %collective-permute-start.4 = (bf16[1,1440,768]{2,1,0:T(8,128)(2,1)}, bf16[1,1440,768]{2,1,0:T(8,128)(2,1)}, u32[]{:S(2)}, u32[]{:S(2)}) collective-permute-start(bf16[1,1440,768]{2,1,0:T(8,128)(2,1)} %all-gather.2.cloned.1.call-done), channel_id=1, source_target_pairs={{0,4},{4,8},{8,12},{12,16},{16,20},{20,24},{24,28},{28,32},{32,36}... | collective-permute-start | bytes 6635528 | tf_op jit(solution)/shard_map/ppermute | solution.py:20
  103.6 21.4 %collective-permute-done.4 = bf16[1,1440,768]{2,1,0:T(8,128)(2,1)} collective-permute-done((bf16[1,1440,768]{2,1,0:T(8,128)(2,1)}, bf16[1,1440,768]{2,1,0:T(8,128)(2,1)}, u32[]{:S(2)}, u32[]{:S(2)}) %collective-permute-start.4) | collective-permute-done | bytes 2211872 | tf_op jit(solution)/shard_map/ppermute | solution.py:20
  126.9 6.7 %collective-permute-done.5 = bf16[1,1440,768]{2,1,0:T(8,128)(2,1)} collective-permute-done((bf16[1,1440,768]{2,1,0:T(8,128)(2,1)}, bf16[1,1440,768]{2,1,0:T(8,128)(2,1)}, u32[]{:S(2)}, u32[]{:S(2)}) %collective-permute-start.5) | collective-permute-done | bytes 2211872 | tf_op jit(solution)/shard_map/ppermute | solution.py:23
  135.4 3.4 %fusion.90 = (bf16[3,1440,384]{2,1,0:T(8,128)(2,1)}, bf16[3,1440,384]{2,1,0:T(8,128)(2,1)}) fusion(bf16[3,1440,768]{2,1,0:T(8,128)(2,1)S(1)} %constant_dynamic-update-slice_fusion.51), kind=kLoop, calls=%fused_computation.220 | loop fusion | bytes 13271040 | tf_op jit(solution)/shard_map/slice | solution.py:108
  138.8 8.6 %copy.1533 = bf16[3,1440,384]{1,0,2:T(4,128)(2,1)} copy(bf16[3,1440,384]{2,1,0:T(8,128)(2,1)} %get-tuple-element.308) | data formatting | bytes 6635520 | tf_op jit(solution)/shard_map/slice | solution.py:107
  147.4 9.8 %reshape_reshape.7 = bf16[4320,8,48]{0,2,1:T(8,128)(2,1)} reshape(bf16[3,1440,384]{1,0,2:T(4,128)(2,1)} %copy.1533) | data formatting | bytes 6635520 | tf_op jit(solution)/shard_map/reshape;reshape | solution.py:111
  157.2 8.6 %copy.1534 = bf16[3,1440,384]{1,0,2:T(4,128)(2,1)} copy(bf16[3,1440,384]{2,1,0:T(8,128)(2,1)} %get-tuple-element.307) | data formatting | bytes 6635520 | tf_op jit(solution)/shard_map/slice | solution.py:108
  165.9 9.9 %reshape_reshape.8 = bf16[4320,8,48]{0,2,1:T(8,128)(2,1)} reshape(bf16[3,1440,384]{1,0,2:T(4,128)(2,1)} %copy.1534) | data formatting | bytes 6635520 | tf_op jit(solution)/shard_map/reshape;reshape | solution.py:112
  175.8 54.0 %while.11 = (s32[]{:T(128)}, bf16[8,360,48]{1,2,0:T(8,128)(2,1)S(1)}, bf16[8,360,48]{1,2,0:T(8,128)(2,1)S(1)}, bf16[8,4320,48]{1,2,0:T(8,128)(2,1)}, f32[8]{0:T(...) while((s32[]{:T(128)}, ...), condition=%wide.region_4.5_spmd.clone, body=%wide.region_1.4_spmd.clone.sunk | while | flops 309501376 | bytes 19683840 | solution.py:126
  177.2 2.1 fusion.103
  180.3 2.2 fusion.105
  184.0 2.1 fusion.103
  187.1 2.2 fusion.105
  193.8 2.2 fusion.105
  200.6 2.2 fusion.105
  207.3 2.2 fusion.105
  214.1 2.2 fusion.105
  220.8 2.2 fusion.105
  227.6 2.2 fusion.105
  (142 shorter events, 58.0 us)
Async XLA Ops:
  6.5 32.2 %copy-start = (bf16[9,72,384]{2,1,0:T(8,128)(2,1)S(1)}, bf16[9,72,384]{2,1,0:T(8,128)(2,1)}, u32[]{:S(2)}) copy-start(bf16[9,72,384]{2,1,0:T(8,128)(2,1)} %param.14) | copy-start | bytes 1492996
  6.5 25.4 %copy-start.1 = (bf16[1,360,72]{1,2,0:T(8,128)(2,1)S(1)}, bf16[1,360,72]{1,2,0:T(8,128)(2,1)}, u32[]{:S(2)}) copy-start(bf16[1,360,72]{1,2,0:T(8,128)(2,1)} %param.11) | copy-start | bytes 155524
  6.5 88.7 %all-gather.2.cloned.1.call-start = ((), (), s32[]{:S(2)}) async-start(), calls=%async_computation | async-start | bytes 2764800 | tf_op jit(solution)/shard_map/all_gather | solution.py:51
  7.4 9.5 %collective-permute-start = (bf16[1,8,72]{1,2,0:T(8,128)(2,1)S(1)}, bf16[1,8,72]{1,2,0:T(8,128)(2,1)S(1)}, u32[]{:S(2)}, u32[]{:S(2)}) collective-permute-start(bf16[1,8,72]{1,2,0:T(8,128)(2,1)S(1)} %get-tuple-element.317), channel_id=1, source_target_pairs={{0,1},{1,2},{2,3},{3,0},{4,5},{5,6},{6,7},{7,4},{8,9},{9,10},{10,1... | collective-permute-start | bytes 3464 | tf_op jit(solution)/shard_map/ppermute | solution.py:20
  10.4 6.5 %collective-permute-start.1 = (bf16[1,8,72]{1,2,0:T(8,128)(2,1)S(1)}, bf16[1,8,72]{1,2,0:T(8,128)(2,1)S(1)}, u32[]{:S(2)}, u32[]{:S(2)}) collective-permute-start(bf16[1,8,72]{1,2,0:T(8,128)(2,1)S(1)} %get-tuple-element.318), channel_id=1, source_target_pairs={{1,0},{2,1},{3,2},{0,3},{5,4},{6,5},{7,6},{4,7},{9,8},{10,9},{11,1... | collective-permute-start | bytes 3464 | tf_op jit(solution)/shard_map/ppermute | solution.py:23
  17.9 15.0 %collective-permute-start.2 = (bf16[1,376,72]{1,2,0:T(8,128)(2,1)S(1)}, bf16[1,376,72]{1,2,0:T(8,128)(2,1)S(1)}, u32[]{:S(2)}, u32[]{:S(2)}) collective-permute-start(bf16[1,376,72]{1,2,0:T(8,128)(2,1)S(1)} %pad_maximum_fusion.4), channel_id=1, source_target_pairs={{0,4},{4,8},{8,12},{12,16},{16,20},{20,24},{24,28},{28,32},{32,36}... | collective-permute-start | bytes 162440 | tf_op jit(solution)/shard_map/ppermute | solution.py:20
  21.0 13.7 %collective-permute-start.3 = (bf16[1,376,72]{1,2,0:T(8,128)(2,1)S(1)}, bf16[1,376,72]{1,2,0:T(8,128)(2,1)S(1)}, u32[]{:S(2)}, u32[]{:S(2)}) collective-permute-start(bf16[1,376,72]{1,2,0:T(8,128)(2,1)S(1)} %pad_maximum_fusion.4), channel_id=1, source_target_pairs={{4,0},{8,4},{12,8},{16,12},{20,16},{24,20},{28,24},{32,28},{36,32}... | collective-permute-start | bytes 162440 | tf_op jit(solution)/shard_map/ppermute | solution.py:23
  38.8 0.7 copy-start.5
  40.4 62.2 %copy-start.6 = (s32[1,1,3,4]{3,1,2,0:T(1,128)S(1)}, s32[1,1,3,4]{3,1,2,0:T(1,128)}, u32[]{:S(2)}) copy-start(s32[1,1,3,4]{3,1,2,0:T(1,128)} %param.19) | copy-start | bytes 148
  95.3 31.5 %copy-start.2 = (bf16[1,1440,768]{2,1,0:T(8,128)(2,1)S(1)}, bf16[1,1440,768]{2,1,0:T(8,128)(2,1)}, u32[]{:S(2)}) copy-start(bf16[1,1440,768]{2,1,0:T(8,128)(2,1)} %all-gather.2.cloned.1.call-done) | copy-start | bytes 6635524
  95.3 29.7 %collective-permute-start.4 = (bf16[1,1440,768]{2,1,0:T(8,128)(2,1)}, bf16[1,1440,768]{2,1,0:T(8,128)(2,1)}, u32[]{:S(2)}, u32[]{:S(2)}) collective-permute-start(bf16[1,1440,768]{2,1,0:T(8,128)(2,1)} %all-gather.2.cloned.1.call-done), channel_id=1, source_target_pairs={{0,4},{4,8},{8,12},{12,16},{16,20},{20,24},{24,28},{28,32},{32,36}... | collective-permute-start | bytes 6635528 | tf_op jit(solution)/shard_map/ppermute | solution.py:20
  100.5 33.1 %collective-permute-start.5 = (bf16[1,1440,768]{2,1,0:T(8,128)(2,1)}, bf16[1,1440,768]{2,1,0:T(8,128)(2,1)}, u32[]{:S(2)}, u32[]{:S(2)}) collective-permute-start(bf16[1,1440,768]{2,1,0:T(8,128)(2,1)} %all-gather.2.cloned.1.call-done), channel_id=1, source_target_pairs={{4,0},{8,4},{12,8},{16,12},{20,16},{24,20},{28,24},{32,28},{36,32}... | collective-permute-start | bytes 6635528 | tf_op jit(solution)/shard_map/ppermute | solution.py:23
  165.9 9.9 %copy-start.4 = (bf16[8,360,48]{1,2,0:T(8,128)(2,1)S(1)}, bf16[8,360,48]{1,2,0:T(8,128)(2,1)}, u32[]{:S(2)}) copy-start(bf16[8,360,48]{1,2,0:T(8,128)(2,1)} %custom-call.4) | copy-start | bytes 829444
  165.9 9.9 %copy-start.7 = (f32[8]{0:T(128)S(1)}, f32[8]{0:T(128)}, u32[]{:S(2)}) copy-start(f32[8]{0:T(128)} %param.18) | copy-start | bytes 100
  175.8 54.0 %copy-start.3 = (bf16[384,384]{1,0:T(8,128)(2,1)S(1)}, bf16[384,384]{1,0:T(8,128)(2,1)}, u32[]{:S(2)}) copy-start(bf16[384,384]{1,0:T(8,128)(2,1)} %param.17) | copy-start | bytes 884740
Sparse Core Ops, SparseCore 0:
  42.6 52.6 all-gather.1
where the time goes:
time: 240 us; the launch traced here: 238 us
  waiting for transfers between devices  80.9 us (34%)
  local copies, waits for them, and re-layouts  58.4 us (24%)
  matrix products  39.3 us (16%)
  other arithmetic  20.6 us (9%)
  starting transfers between devices  18.4 us (8%)
  between operations  14.6 us (6%)
  loops' own time  5.43 us (2%)
    all_gather x1, waiting for transfers between devices, spread(): cycle_cells = lax.all_gather(payload, 'sector', axis=1, tiled=True)  52.8 us
    ppermute x3, waiting for transfers between devices, padded(): lax.ppermute(lax.slice_in_dim(block, block.shape[dim] - width, None, axis...  21.4 us
    dot_general x8, matrix products, one_head(): jnp.dot(expo.astype(jnp.bfloat16), v_head, preferred_element_type=jnp.flo...  17.4 us
    dot_general x8, matrix products, one_head(): jnp.einsum('qd,kd->qk', q_head, k_head, preferred_element_type=jnp.float32)  17 us
    slice x2, local copies, waits for them, and re-layouts, local(): value_all = gathered[..., d_model:].reshape(key_rows, nlon, HEADS, head_dim)  12.1 us
    ppermute x3, starting transfers between devices, padded(): lax.ppermute(lax.slice_in_dim(block, block.shape[dim] - width, None, axis...  11.3 us
    another operation x1, local copies, waits for them, and re-layouts, local(): value_all.reshape(key_rows * nlon, HEADS, head_dim)  9.86 us
    another operation x1, local copies, waits for them, and re-layouts, local(): key_all.reshape(key_rows * nlon, HEADS, head_dim)  9.81 us
  transfers between devices with their start and end apart: 7, of which 3 were waited for; matrix products, arithmetic and copies ran while one was open for 7% of the time, Pallas kernels for 0%

commit v1 on v0

--- a/solution.py
+++ b/solution.py
@@ -48,7 +48,10 @@
 
 
 def spread(payload):
-    cycle_cells = lax.all_gather(payload, "sector", axis=1, tiled=True)
+    size = lax.axis_size("sector")
+    blocks = jnp.stack([payload for _ in range(size)])
+    blocks = lax.all_to_all(blocks, "sector", split_axis=0, concat_axis=0)
+    cycle_cells = jnp.concatenate(blocks, axis=1)
     return padded(cycle_cells, (("band", 0),), KH, False)
 
 

time: 240 us -> 231 us (0.963)
  blocking collectives: 0 us -> 56.6 us
  waiting for transfers between devices: 80.9 us -> 29.8 us
  between operations: 14.6 us -> 1.23 us
  local copies, waits for them, and re-layouts: 58.4 us -> 54.1 us
  other arithmetic: 20.6 us -> 23.8 us
    all_to_all x0 -> x1, blocking collectives: none -> 56.6 us  [spread(): blocks = lax.all_to_all(blocks, 'sector', split_axis=0, concat_axis=0)]
    all_gather x1 -> x0, waiting for transfers between devices: 52.8 us -> none  [spread(): cycle_cells = lax.all_gather(payload, 'sector', axis=1, tiled=True)]
    concatenate x1 -> x2, other arithmetic: 0.91 us -> 4.13 us  [padded(): block = jnp.concatenate([low, block, high], axis=dim)]
    unnamed x53 -> x49, local copies, waits for them, and re-layouts: 7.28 us -> 5.37 us
  transfers between devices with their start and end apart: 7 -> 6, of which waited for: 3 -> 2; matrix products, arithmetic and copies ran while one was open for 7% -> 7% of each run, Pallas kernels for 0% -> 0%
where the time goes in v1:
time: 231 us; the launch traced here: 228 us
  blocking collectives  56.6 us (25%)
  local copies, waits for them, and re-layouts  54.1 us (23%)
  matrix products  39.3 us (17%)
  waiting for transfers between devices  29.8 us (13%)
  other arithmetic  23.8 us (10%)
  starting transfers between devices  17.9 us (8%)
  loops' own time  5.43 us (2%)
    all_to_all x1, blocking collectives, spread(): blocks = lax.all_to_all(blocks, 'sector', split_axis=0, concat_axis=0)  56.6 us
    ppermute x3, waiting for transfers between devices, padded(): lax.ppermute(lax.slice_in_dim(block, block.shape[dim] - width, None, axis...  21.1 us
    dot_general x8, matrix products, one_head(): jnp.dot(expo.astype(jnp.bfloat16), v_head, preferred_element_type=jnp.flo...  17.4 us
    dot_general x8, matrix products, one_head(): jnp.einsum('qd,kd->qk', q_head, k_head, preferred_element_type=jnp.float32)  17 us
    slice x2, local copies, waits for them, and re-layouts, local(): value_all = gathered[..., d_model:].reshape(key_rows, nlon, HEADS, head_dim)  12.1 us
    ppermute x3, starting transfers between devices, padded(): lax.ppermute(lax.slice_in_dim(block, block.shape[dim] - width, None, axis...  10.8 us
    another operation x1, local copies, waits for them, and re-layouts, local(): value_all.reshape(key_rows * nlon, HEADS, head_dim)  9.92 us
    another operation x1, local copies, waits for them, and re-layouts, local(): key_all.reshape(key_rows * nlon, HEADS, head_dim)  9.81 us
  transfers between devices with their start and end apart: 6, of which 2 were waited for; matrix products, arithmetic and copies ran while one was open for 7% of the time, Pallas kernels for 0%

profile of v1, /device:TPU:31, one launch (start us, length us, event | category | flops | bytes accessed | tf_op | source)
XLA Modules:
  0.0 228.2 jit_solution(3920541457991879861)
XLA Ops:
  0.9 3.0 %collective-permute-start = (bf16[1,8,72]{1,2,0:T(8,128)(2,1)S(1)}, bf16[1,8,72]{1,2,0:T(8,128)(2,1)S(1)}, u32[]{:S(2)}, u32[]{:S(2)}) collective-permute-start(bf16[1,8,72]{1,2,0:T(8,128)(2,1)S(1)} %get-tuple-element.317), channel_id=1, source_target_pairs={{0,1},{1,2},{2,3},{3,0},{4,5},{5,6},{6,7},{7,4},{8,9},{9,10},{10,1... | collective-permute-start | bytes 3464 | tf_op jit(solution)/shard_map/ppermute | solution.py:20
  3.9 3.1 %collective-permute-start.1 = (bf16[1,8,72]{1,2,0:T(8,128)(2,1)S(1)}, bf16[1,8,72]{1,2,0:T(8,128)(2,1)S(1)}, u32[]{:S(2)}, u32[]{:S(2)}) collective-permute-start(bf16[1,8,72]{1,2,0:T(8,128)(2,1)S(1)} %get-tuple-element.318), channel_id=1, source_target_pairs={{1,0},{2,1},{3,2},{0,3},{5,4},{6,5},{7,6},{4,7},{9,8},{10,9},{11,1... | collective-permute-start | bytes 3464 | tf_op jit(solution)/shard_map/ppermute | solution.py:23
  11.4 3.1 %collective-permute-start.2 = (bf16[1,376,72]{1,2,0:T(8,128)(2,1)S(1)}, bf16[1,376,72]{1,2,0:T(8,128)(2,1)S(1)}, u32[]{:S(2)}, u32[]{:S(2)}) collective-permute-start(bf16[1,376,72]{1,2,0:T(8,128)(2,1)S(1)} %pad_maximum_fusion.4), channel_id=1, source_target_pairs={{0,4},{4,8},{8,12},{12,16},{16,20},{20,24},{24,28},{28,32},{32,36}... | collective-permute-start | bytes 162440 | tf_op jit(solution)/shard_map/ppermute | solution.py:20
  29.9 2.3 %fusion.30 = bf16[9,360,72]{1,0,2:T(8,128)(2,1)S(1)} fusion(bf16[1,1,17,360,72]{3,2,1,4,0:T(8,128)(2,1)S(1)} %bitcast.323, bf16[1,1,17,360,72]{3,2,1,4,0:T(8,128)(2,1)S(1)} %bitcast.321, bf16[1,1,17,360,72]{3,2,1,4,0:T(8,128)(2,1)S(1)} %bitcast.322, f32[9,1,3,17]{3,1,2,0:T(1,128)S(1)} %broadcast_multiply_fusion), kind=kOutput, calls=%fused_computation.31 | convolution fusion | flops 145644480 | bytes 3112236 | tf_op jit(solution)/shard_map/kiab,iabjc->kijc/dot_general | solution.py:84
  35.2 56.6 %all_to_all.5 = bf16[4,1,360,768]{3,2,1,0:T(8,128)(2,1)S(1)} all-to-all(bf16[4,1,360,768]{3,2,1,0:T(8,128)(2,1)S(1)} %stack.239), channel_id=1, replica_groups=mesh['band'=64,'sector'=4] {'sector'}, dimensions={0} | all-to-all | bytes 4423680 | tf_op jit(solution)/shard_map/all_to_all | solution.py:53
  91.8 4.7 %collective-permute-start.4 = (bf16[1,1440,768]{2,1,0:T(8,128)(2,1)S(1)}, bf16[1,1440,768]{2,1,0:T(8,128)(2,1)}, u32[]{:S(2)}, u32[]{:S(2)}) collective-permute-start(bf16[1,1440,768]{2,1,0:T(8,128)(2,1)S(1)} %bitcast.315), channel_id=1, source_target_pairs={{0,4},{4,8},{8,12},{12,16},{16,20},{20,24},{24,28},{28,32},{32,36}... | collective-permute-start | bytes 6635528 | tf_op jit(solution)/shard_map/ppermute | solution.py:20
  99.6 21.1 %collective-permute-done.4 = bf16[1,1440,768]{2,1,0:T(8,128)(2,1)} collective-permute-done((bf16[1,1440,768]{2,1,0:T(8,128)(2,1)S(1)}, bf16[1,1440,768]{2,1,0:T(8,128)(2,1)}, u32[]{:S(2)}, u32[]{:S(2)}) %collective-permute-start.4) | collective-permute-done | bytes 2211872 | tf_op jit(solution)/shard_map/ppermute | solution.py:20
  120.7 8.7 %collective-permute-done.5 = bf16[1,1440,768]{2,1,0:T(8,128)(2,1)} collective-permute-done((bf16[1,1440,768]{2,1,0:T(8,128)(2,1)S(1)}, bf16[1,1440,768]{2,1,0:T(8,128)(2,1)}, u32[]{:S(2)}, u32[]{:S(2)}) %collective-permute-start.5) | collective-permute-done | bytes 2211872 | tf_op jit(solution)/shard_map/ppermute | solution.py:23
  129.4 3.2 %pad_maximum_fusion = bf16[3,1440,768]{2,1,0:T(8,128)(2,1)S(1)} fusion(bf16[1,1440,768]{2,1,0:T(8,128)(2,1)} %collective-permute-done.5, bf16[1,1440,768]{2,1,0:T(8,128)(2,1)S(1)} %bitcast.317, bf16[1,1440,768]{2,1,0:T(8,128)(2,1)} %collective-permute-done.4), kind=kLoop, calls=%fused_computation.19 | loop fusion | flops 6635520 | bytes 13271040 | tf_op jit(solution)/shard_map/concatenate | solution.py:24
  132.7 3.5 %fusion.90 = (bf16[3,1440,384]{2,1,0:T(8,128)(2,1)}, bf16[3,1440,384]{2,1,0:T(8,128)(2,1)}) fusion(bf16[3,1440,768]{2,1,0:T(8,128)(2,1)S(1)} %pad_maximum_fusion), kind=kLoop, calls=%fused_computation.218 | loop fusion | bytes 13271040 | tf_op jit(solution)/shard_map/slice | solution.py:111
  136.1 8.6 %copy.1562 = bf16[3,1440,384]{1,0,2:T(4,128)(2,1)} copy(bf16[3,1440,384]{2,1,0:T(8,128)(2,1)} %get-tuple-element.308) | data formatting | bytes 6635520 | tf_op jit(solution)/shard_map/slice | solution.py:110
  144.8 9.8 %reshape_reshape.7 = bf16[4320,8,48]{0,2,1:T(8,128)(2,1)} reshape(bf16[3,1440,384]{1,0,2:T(4,128)(2,1)} %copy.1562) | data formatting | bytes 6635520 | tf_op jit(solution)/shard_map/reshape;reshape | solution.py:114
  154.6 8.6 %copy.1563 = bf16[3,1440,384]{1,0,2:T(4,128)(2,1)} copy(bf16[3,1440,384]{2,1,0:T(8,128)(2,1)} %get-tuple-element.307) | data formatting | bytes 6635520 | tf_op jit(solution)/shard_map/slice | solution.py:111
  163.2 9.9 %reshape_reshape.8 = bf16[4320,8,48]{0,2,1:T(8,128)(2,1)} reshape(bf16[3,1440,384]{1,0,2:T(4,128)(2,1)} %copy.1563) | data formatting | bytes 6635520 | tf_op jit(solution)/shard_map/reshape;reshape | solution.py:115
  173.1 54.0 %while.11 = (s32[]{:T(128)}, bf16[8,360,48]{1,2,0:T(8,128)(2,1)S(1)}, bf16[8,360,48]{1,2,0:T(8,128)(2,1)S(1)}, bf16[8,4320,48]{1,2,0:T(8,128)(2,1)}, f32[8]{0:T(...) while((s32[]{:T(128)}, ...), condition=%wide.region_4.5_spmd.clone, body=%wide.region_1.4_spmd.clone.sunk | while | flops 309501376 | bytes 19683840 | solution.py:129
  177.7 2.2 fusion.105
  181.3 2.1 fusion.103
  184.4 2.2 fusion.105
  191.2 2.2 fusion.105
  197.9 2.2 fusion.105
  204.7 2.2 fusion.105
  211.4 2.2 fusion.105
  218.1 2.2 fusion.105
  224.9 2.2 fusion.105
  (137 shorter events, 55.8 us)
Async XLA Ops:
  0.0 32.2 %copy-start = (bf16[9,72,384]{2,1,0:T(8,128)(2,1)S(1)}, bf16[9,72,384]{2,1,0:T(8,128)(2,1)}, u32[]{:S(2)}) copy-start(bf16[9,72,384]{2,1,0:T(8,128)(2,1)} %param.14) | copy-start | bytes 1492996
  0.0 25.4 %copy-start.1 = (bf16[1,360,72]{1,2,0:T(8,128)(2,1)S(1)}, bf16[1,360,72]{1,2,0:T(8,128)(2,1)}, u32[]{:S(2)}) copy-start(bf16[1,360,72]{1,2,0:T(8,128)(2,1)} %param.11) | copy-start | bytes 155524
  0.9 9.5 %collective-permute-start = (bf16[1,8,72]{1,2,0:T(8,128)(2,1)S(1)}, bf16[1,8,72]{1,2,0:T(8,128)(2,1)S(1)}, u32[]{:S(2)}, u32[]{:S(2)}) collective-permute-start(bf16[1,8,72]{1,2,0:T(8,128)(2,1)S(1)} %get-tuple-element.317), channel_id=1, source_target_pairs={{0,1},{1,2},{2,3},{3,0},{4,5},{5,6},{6,7},{7,4},{8,9},{9,10},{10,1... | collective-permute-start | bytes 3464 | tf_op jit(solution)/shard_map/ppermute | solution.py:20
  3.9 6.5 %collective-permute-start.1 = (bf16[1,8,72]{1,2,0:T(8,128)(2,1)S(1)}, bf16[1,8,72]{1,2,0:T(8,128)(2,1)S(1)}, u32[]{:S(2)}, u32[]{:S(2)}) collective-permute-start(bf16[1,8,72]{1,2,0:T(8,128)(2,1)S(1)} %get-tuple-element.318), channel_id=1, source_target_pairs={{1,0},{2,1},{3,2},{0,3},{5,4},{6,5},{7,6},{4,7},{9,8},{10,9},{11,1... | collective-permute-start | bytes 3464 | tf_op jit(solution)/shard_map/ppermute | solution.py:23
  11.4 15.0 %collective-permute-start.2 = (bf16[1,376,72]{1,2,0:T(8,128)(2,1)S(1)}, bf16[1,376,72]{1,2,0:T(8,128)(2,1)S(1)}, u32[]{:S(2)}, u32[]{:S(2)}) collective-permute-start(bf16[1,376,72]{1,2,0:T(8,128)(2,1)S(1)} %pad_maximum_fusion.4), channel_id=1, source_target_pairs={{0,4},{4,8},{8,12},{12,16},{16,20},{20,24},{24,28},{28,32},{32,36}... | collective-permute-start | bytes 162440 | tf_op jit(solution)/shard_map/ppermute | solution.py:20
  14.4 13.7 %collective-permute-start.3 = (bf16[1,376,72]{1,2,0:T(8,128)(2,1)S(1)}, bf16[1,376,72]{1,2,0:T(8,128)(2,1)S(1)}, u32[]{:S(2)}, u32[]{:S(2)}) collective-permute-start(bf16[1,376,72]{1,2,0:T(8,128)(2,1)S(1)} %pad_maximum_fusion.4), channel_id=1, source_target_pairs={{4,0},{8,4},{12,8},{16,12},{20,16},{24,20},{28,24},{32,28},{36,32}... | collective-permute-start | bytes 162440 | tf_op jit(solution)/shard_map/ppermute | solution.py:23
  32.2 0.7 copy-start.4
  35.1 63.6 %copy-start.5 = (s32[1,1,3,4]{3,1,2,0:T(1,128)S(1)}, s32[1,1,3,4]{3,1,2,0:T(1,128)}, u32[]{:S(2)}) copy-start(s32[1,1,3,4]{3,1,2,0:T(1,128)} %param.19) | copy-start | bytes 148
  91.8 28.9 %collective-permute-start.4 = (bf16[1,1440,768]{2,1,0:T(8,128)(2,1)S(1)}, bf16[1,1440,768]{2,1,0:T(8,128)(2,1)}, u32[]{:S(2)}, u32[]{:S(2)}) collective-permute-start(bf16[1,1440,768]{2,1,0:T(8,128)(2,1)S(1)} %bitcast.315), channel_id=1, source_target_pairs={{0,4},{4,8},{8,12},{12,16},{16,20},{20,24},{24,28},{28,32},{32,36}... | collective-permute-start | bytes 6635528 | tf_op jit(solution)/shard_map/ppermute | solution.py:20
  96.5 32.9 %collective-permute-start.5 = (bf16[1,1440,768]{2,1,0:T(8,128)(2,1)S(1)}, bf16[1,1440,768]{2,1,0:T(8,128)(2,1)}, u32[]{:S(2)}, u32[]{:S(2)}) collective-permute-start(bf16[1,1440,768]{2,1,0:T(8,128)(2,1)S(1)} %bitcast.316), channel_id=1, source_target_pairs={{4,0},{8,4},{12,8},{16,12},{20,16},{24,20},{28,24},{32,28},{36,32}... | collective-permute-start | bytes 6635528 | tf_op jit(solution)/shard_map/ppermute | solution.py:23
  163.2 9.9 %copy-start.3 = (bf16[8,360,48]{1,2,0:T(8,128)(2,1)S(1)}, bf16[8,360,48]{1,2,0:T(8,128)(2,1)}, u32[]{:S(2)}) copy-start(bf16[8,360,48]{1,2,0:T(8,128)(2,1)} %custom-call.3) | copy-start | bytes 829444
  163.2 9.9 %copy-start.6 = (f32[8]{0:T(128)S(1)}, f32[8]{0:T(128)}, u32[]{:S(2)}) copy-start(f32[8]{0:T(128)} %param.18) | copy-start | bytes 100
  173.1 54.0 %copy-start.2 = (bf16[384,384]{1,0:T(8,128)(2,1)S(1)}, bf16[384,384]{1,0:T(8,128)(2,1)}, u32[]{:S(2)}) copy-start(bf16[384,384]{1,0:T(8,128)(2,1)} %param.17) | copy-start | bytes 884740
